TPU v7x, 32 devices: a whole 2x2x4 slice. The times are simulated.
32 devices in a mesh: segment: 4 (over y, x), dom: 8 (over z, core).
Axes of the slice: x: 2, y: 2, z: 4, core: 2. Of those that a mesh axis runs over, the one named last changes fastest.
Arguments:
- features: bfloat16 [4, 4096, 512], P(None, 'dom'), may hold values from -6 to 6
- send_rows: int32 [4, 8, 8, 128], P(None, 'dom'), may hold values from 0 to 511
- send_len: int32 [4, 8, 8], P(None, 'dom'), may hold values from 0 to 128, as said below
- tile_src: int32 [4, 32, 4], P(None, 'dom'), may hold values from 0 to 11
- tile_count: int32 [4, 32], P(None, 'dom'), may hold values from 1 to 4, as said below
- tile_val: bfloat16 [4, 32, 4, 128, 128], P(None, 'dom'), may hold values from -0.25 to 0.25
- w_self: bfloat16 [4, 512, 512], P('segment'), may hold values from -0.25 to 0.25
- w_neigh: bfloat16 [4, 512, 512], P('segment'), may hold values from -0.25 to 0.25
- gain: bfloat16 [4, 512], P('segment'), may hold values from 0.25 to 1.75
- bias: bfloat16 [4, 512], P('segment'), may hold values from -3 to 3
Outputs:
- acts: bfloat16 [4, 4, 4096, 512], P('segment', None, 'dom')
Inputs may be any that keep to these rules, and one draw needn't show every extreme that they name: `send_len`: A partition sends nothing to itself; in every span each partition sends a full block of 128 rows to one other partition. `tile_count`: in every span one partition has 4 live tiles in each of its blocks.
All inputs are finite; a program needn't handle non-finite values.
Results may differ from a plain program's by a relative error of at most 0.0065.
Values may be sent and summed in bfloat16 or wider, within the bound.
No kernel may reach another device: no remote copies, remote signals or barrier semaphores. Data moves between devices by JAX's collectives and lax.ppermute only.
A program may use at most 64 MiB of HBM per device.

v0:
```python
import jax
import jax.numpy as jnp
from jax import lax
from jax.sharding import PartitionSpec as P

norm_eps = 1e-05


def select_span(array_in, span_id):
    return lax.dynamic_index_in_dim(array_in, span_id, 0, keepdims=False)


def sage_layer(inputs, span_id, graph, w_one, w_two, gain_one, bias_one):
    rows_all, lens_all, src_all, count_all, vals_all = graph
    send_list = select_span(rows_all, span_id)[0]
    send_count = select_span(lens_all, span_id)[0]
    tile_index = select_span(src_all, span_id)
    tile_total = select_span(count_all, span_id)
    tile_vals = select_span(vals_all, span_id)
    peer_count, tile_rows = send_list.shape
    feat_width = inputs.shape[1]
    block_count, tile_depth = tile_index.shape
    picked = jnp.take(inputs, send_list.reshape(-1), axis=0).reshape(
        peer_count, tile_rows, feat_width
    )
    row_live = lax.broadcasted_iota(jnp.int32, (peer_count, tile_rows), 1) < send_count[:, None]
    outgoing = jnp.where(row_live[:, :, None], picked, jnp.zeros_like(picked))
    incoming = lax.all_to_all(outgoing, "dom", split_axis=0, concat_axis=0, tiled=True)
    sources = jnp.concatenate(
        [inputs.reshape(block_count, tile_rows, feat_width), incoming], axis=0
    )
    tile_live = lax.broadcasted_iota(jnp.int32, (block_count, tile_depth), 1) < tile_total[:, None]

    def block_sum(packed):
        block_index, block_vals, block_live = packed
        chosen = jnp.take(sources, block_index, axis=0)
        masked = jnp.where(block_live[:, None, None], block_vals, jnp.zeros_like(block_vals))
        return jnp.einsum("kij,kjd->id", masked, chosen, preferred_element_type=jnp.float32)

    summed = lax.map(block_sum, (tile_index, tile_vals, tile_live))
    gathered = summed.reshape(block_count * tile_rows, feat_width).astype(jnp.bfloat16)
    mixed = jnp.dot(inputs, w_one, preferred_element_type=jnp.float32) + jnp.dot(
        gathered, w_two, preferred_element_type=jnp.float32
    )
    center = mixed - jnp.mean(mixed, axis=1, keepdims=True)
    spread = jnp.mean(center * center, axis=1, keepdims=True)
    scaled = center * lax.rsqrt(spread + norm_eps) * gain_one.astype(jnp.float32) + bias_one.astype(
        jnp.float32
    )
    return jnp.maximum(scaled, 0.0).astype(jnp.bfloat16)


def per_device(
    features, send_rows, send_len, tile_src, tile_count, tile_val, w_self, w_neigh, gain, bias
):
    segments = lax.axis_size("segment")
    segment_id = lax.axis_index("segment")
    span_total, node_rows, feat_width = features.shape
    graph = (send_rows, send_len, tile_src, tile_count, tile_val)
    every_self, every_neigh, every_gain, every_bias = (
        lax.all_gather(w_self, "segment", axis=0, tiled=True),
        lax.all_gather(w_neigh, "segment", axis=0, tiled=True),
        lax.all_gather(gain, "segment", axis=0, tiled=True),
        lax.all_gather(bias, "segment", axis=0, tiled=True),
    )
    span_group = span_total // segments
    layers = every_self.shape[0]
    span_id = segment_id * span_group + 0
    hidden = select_span(features, span_id)
    outputs = []
    for layer_id in range(layers):
        hidden = sage_layer(
            hidden,
            span_id,
            graph,
            every_self[layer_id],
            every_neigh[layer_id],
            every_gain[layer_id],
            every_bias[layer_id],
        )
        outputs.append(hidden)
    finished = [jnp.stack(outputs)]
    dealt_out = jnp.stack(finished, axis=1)
    return lax.all_to_all(dealt_out, "segment", split_axis=0, concat_axis=1, tiled=True)


def solution(mesh):
    in_specs = (
        P(None, "dom", None),
        P(None, "dom", None, None),
        P(None, "dom", None),
        P(None, "dom", None),
        P(None, "dom"),
        P(None, "dom", None, None, None),
        P("segment", None, None),
        P("segment", None, None),
        P("segment", None),
        P("segment", None),
    )
    out_specs = P("segment", None, "dom", None)
    return jax.shard_map(
        per_device, mesh=mesh, in_specs=in_specs, out_specs=out_specs, check_vma=False
    )
```

profile of v0, /device:TPU:0, one launch (start us, length us, event | category | flops | bytes accessed | tf_op | source)
XLA Modules:
  0.0 296.5 jit_solution(8535459585677246511)
XLA Ops:
  8.2 5.1 %gather_fusion.4 = bf16[1024,512]{1,0:T(8,128)(2,1)} fusion(bf16[512,512]{1,0:T(8,128)(2,1)S(1)} %fusion.67, s32[1024]{0:T(1024)S(1)} %fusion.49), kind=kCustom, calls=%fused_computation.clone | custom fusion | bytes 2101248 | tf_op jit(solution)/shard_map/jit(_take)/gather | solution.py:23
  17.3 6.5 %all-to-all-start = ((bf16[8,128,512]{2,1,0:T(8,128)(2,1)}), bf16[8,128,512]{2,1,0:T(8,128)(2,1)}, u32[]{:S(2)}, u32[]{:S(2)}) async-start(bf16[8,128,512]{2,1,0:T(8,128)(2,1)} %broadcast_select_fusion.7), calls=%async_computation | async-start | bytes 2097152 | tf_op jit(solution)/shard_map/all_to_all | solution.py:28
  24.5 8.1 %all-gather = bf16[4,1,512]{2,1,0:T(2,128)(2,1)S(1)} all-gather(bf16[1,1,512]{2,1,0:T(2,128)(2,1)S(1)} %bitcast.203), channel_id=1, replica_groups=mesh['segment'=4,'dom'=8] {'segment'}, dimensions={0}, use_global_device_ids=true | all-gather | bytes 5120 | tf_op jit(solution)/shard_map/all_gather | solution.py:63
  34.1 8.3 %all-gather.1 = bf16[4,1,512]{2,1,0:T(2,128)(2,1)S(1)} all-gather(bf16[1,1,512]{2,1,0:T(2,128)(2,1)S(1)} %bitcast.204), channel_id=1, replica_groups=mesh['segment'=4,'dom'=8] {'segment'}, dimensions={0}, use_global_device_ids=true | all-gather | bytes 5120 | tf_op jit(solution)/shard_map/all_gather | solution.py:64
  44.3 6.1 %all-to-all-done = bf16[8,128,512]{2,1,0:T(8,128)(2,1)} async-done(((bf16[8,128,512]{2,1,0:T(8,128)(2,1)}), bf16[8,128,512]{2,1,0:T(8,128)(2,1)}, u32[]{:S(2)}, u32[]{:S(2)}) %all-to-all-start) | async-done | bytes 1048608 | tf_op jit(solution)/shard_map/all_to_all | solution.py:28
  50.4 2.5 pad_maximum_fusion
  53.8 15.7 %while.40 = (s32[]{:T(128)}, bf16[4,128,512]{2,1,0:T(8,128)(2,1)}, pred[4,4]{1,0:T(4,128)(4,1)S(1)}, bf16[4,4,128,128]{3,2,1,0:T(8,128)(2,1)}, s32[4,4]{1,0:T(4,...) while((s32[]{:T(128)}, bf16[4,128,512]{2,1,0:T(8,128)(2,1)}, pred[4,4]{1,0:T(4,128)(4,1)S(1)}, ...), condition=%wide.region_1.4_spmd, body=%wide.region_0.3_spmd.sunk | while | flops 67437592 | bytes 1971369 | solution.py:40
  69.5 2.5 fusion.48
  72.0 12.2 %all-gather.7.cloned.1.call-done = bf16[4,512,512]{2,1,0:T(8,128)(2,1)} async-done(((bf16[1,512,512]{2,1,0:T(8,128)(2,1)}), bf16[4,512,512]{2,1,0:T(8,128)(2,1)}) %all-gather.7.cloned.1.call-update) | async-done | bytes 2097168 | tf_op jit(solution)/shard_map/all_gather | solution.py:62
  87.4 5.1 %gather_fusion.5 = bf16[1024,512]{1,0:T(8,128)(2,1)} fusion(bf16[512,512]{1,0:T(8,128)(2,1)S(1)} %maximum_convert_fusion.3, s32[1024]{0:T(1024)S(1)} %fusion.49), kind=kCustom, calls=%fused_computation.2.clone | custom fusion | bytes 2101248 | tf_op jit(solution)/shard_map/jit(_take)/gather | solution.py:23
  95.1 4.6 %all-to-all-start.1 = ((bf16[8,128,512]{2,1,0:T(8,128)(2,1)}), bf16[8,128,512]{2,1,0:T(8,128)(2,1)}, u32[]{:S(2)}, u32[]{:S(2)}) async-start(bf16[8,128,512]{2,1,0:T(8,128)(2,1)} %broadcast_select_fusion.6), calls=%async_computation.1 | async-start | bytes 2097152 | tf_op jit(solution)/shard_map/all_to_all | solution.py:28
  102.2 24.2 %all-to-all-done.1 = bf16[8,128,512]{2,1,0:T(8,128)(2,1)} async-done(((bf16[8,128,512]{2,1,0:T(8,128)(2,1)}), bf16[8,128,512]{2,1,0:T(8,128)(2,1)}, u32[]{:S(2)}, u32[]{:S(2)}) %all-to-all-start.1) | async-done | bytes 1048608 | tf_op jit(solution)/shard_map/all_to_all | solution.py:28
  126.4 2.5 pad_maximum_fusion.1
  128.9 13.2 %while.41 = (s32[]{:T(128)}, bf16[4,128,512]{2,1,0:T(8,128)(2,1)S(1)}, pred[4,4]{1,0:T(4,128)(4,1)S(1)}, bf16[4,4,128,128]{3,2,1,0:T(8,128)(2,1)}, s32[4,4]{1,0:...) while((s32[]{:T(128)}, bf16[4,128,512]{2,1,0:T(8,128)(2,1)S(1)}, pred[4,4]{1,0:T(4,128)(4,1)S(1)}, ...), condition=%wide.region_5.8_spmd, body=%wide.region_4.7_spmd.sunk | while | flops 67437592 | bytes 1972385 | solution.py:40
  145.3 5.1 %gather_fusion.6 = bf16[1024,512]{1,0:T(8,128)(2,1)} fusion(bf16[512,512]{1,0:T(8,128)(2,1)S(1)} %maximum_convert_fusion.2, s32[1024]{0:T(1024)S(1)} %fusion.49), kind=kCustom, calls=%fused_computation.3.clone | custom fusion | bytes 2101248 | tf_op jit(solution)/shard_map/jit(_take)/gather | solution.py:23
  153.0 4.3 %all-to-all-start.2 = ((bf16[8,128,512]{2,1,0:T(8,128)(2,1)}), bf16[8,128,512]{2,1,0:T(8,128)(2,1)}, u32[]{:S(2)}, u32[]{:S(2)}) async-start(bf16[8,128,512]{2,1,0:T(8,128)(2,1)} %broadcast_select_fusion.5), calls=%async_computation.2 | async-start | bytes 2097152 | tf_op jit(solution)/shard_map/all_to_all | solution.py:28
  159.7 24.1 %all-to-all-done.2 = bf16[8,128,512]{2,1,0:T(8,128)(2,1)} async-done(((bf16[8,128,512]{2,1,0:T(8,128)(2,1)}), bf16[8,128,512]{2,1,0:T(8,128)(2,1)}, u32[]{:S(2)}, u32[]{:S(2)}) %all-to-all-start.2) | async-done | bytes 1048608 | tf_op jit(solution)/shard_map/all_to_all | solution.py:28
  183.8 2.5 pad_maximum_fusion.2
  186.3 13.2 %while.42 = (s32[]{:T(128)}, bf16[4,128,512]{2,1,0:T(8,128)(2,1)S(1)}, pred[4,4]{1,0:T(4,128)(4,1)S(1)}, bf16[4,4,128,128]{3,2,1,0:T(8,128)(2,1)}, s32[4,4]{1,0:...) while((s32[]{:T(128)}, bf16[4,128,512]{2,1,0:T(8,128)(2,1)S(1)}, pred[4,4]{1,0:T(4,128)(4,1)S(1)}, ...), condition=%wide.region_9.12_spmd, body=%wide.region_8.11_spmd.sunk | while | flops 67437592 | bytes 1972385 | solution.py:40
  202.7 5.1 %gather_fusion.7 = bf16[1024,512]{1,0:T(8,128)(2,1)} fusion(bf16[512,512]{1,0:T(8,128)(2,1)S(1)} %maximum_convert_fusion.1, s32[1024]{0:T(1024)S(1)} %fusion.49), kind=kCustom, calls=%fused_computation.4.clone | custom fusion | bytes 2101248 | tf_op jit(solution)/shard_map/jit(_take)/gather | solution.py:23
  210.4 4.2 %all-to-all-start.3 = ((bf16[8,128,512]{2,1,0:T(8,128)(2,1)}), bf16[8,128,512]{2,1,0:T(8,128)(2,1)}, u32[]{:S(2)}, u32[]{:S(2)}) async-start(bf16[8,128,512]{2,1,0:T(8,128)(2,1)} %broadcast_select_fusion.4), calls=%async_computation.3 | async-start | bytes 2097152 | tf_op jit(solution)/shard_map/all_to_all | solution.py:28
  221.8 19.4 %all-to-all-done.3 = bf16[8,128,512]{2,1,0:T(8,128)(2,1)} async-done(((bf16[8,128,512]{2,1,0:T(8,128)(2,1)}), bf16[8,128,512]{2,1,0:T(8,128)(2,1)}, u32[]{:S(2)}, u32[]{:S(2)}) %all-to-all-start.3) | async-done | bytes 1048608 | tf_op jit(solution)/shard_map/all_to_all | solution.py:28
  243.8 13.2 %while.43 = (s32[]{:T(128)}, bf16[4,128,512]{2,1,0:T(8,128)(2,1)S(1)}, pred[4,4]{1,0:T(4,128)(4,1)S(1)}, bf16[4,4,128,128]{3,2,1,0:T(8,128)(2,1)}, s32[4,4]{1,0:...) while((s32[]{:T(128)}, bf16[4,128,512]{2,1,0:T(8,128)(2,1)S(1)}, pred[4,4]{1,0:T(4,128)(4,1)S(1)}, ...), condition=%wide.region_13.16_spmd, body=%wide.region_12.15_spmd.sunk | while | flops 67437592 | bytes 1972385 | solution.py:40
  260.5 27.8 %all_to_all.32 = bf16[4,1,512,512]{3,2,1,0:T(8,128)(2,1)S(1)} all-to-all(bf16[4,1,512,512]{3,2,1,0:T(8,128)(2,1)S(1)} %maximum_bitcast_fusion), channel_id=1, replica_groups=mesh['segment'=4,'dom'=8] {'segment'}, dimensions={0} | all-to-all | bytes 4194304 | tf_op jit(solution)/shard_map/all_to_all | solution.py:84
  (162 shorter events, 102.0 us)
Async XLA Ops:
  6.5 1.6 copy-start
  6.5 63.0 %all-gather.5.cloned.1.call-start = ((), (), s32[]{:S(2)}) async-start(), calls=%async_computation.5 | async-start | bytes 2621440 | tf_op jit(solution)/shard_map/all_gather | solution.py:61
  16.1 8.4 %copy-start.10 = (bf16[1,512]{1,0:T(2,128)(2,1)S(1)}, bf16[1,512]{1,0:T(2,128)(2,1)}, u32[]{:S(2)}) copy-start(bf16[1,512]{1,0:T(2,128)(2,1)} %param.30) | copy-start | bytes 3076
  17.3 16.9 %copy-start.11 = (bf16[1,512]{1,0:T(2,128)(2,1)S(1)}, bf16[1,512]{1,0:T(2,128)(2,1)}, u32[]{:S(2)}) copy-start(bf16[1,512]{1,0:T(2,128)(2,1)} %param.31) | copy-start | bytes 3076
  17.3 33.2 %all-to-all-start = ((bf16[8,128,512]{2,1,0:T(8,128)(2,1)}), bf16[8,128,512]{2,1,0:T(8,128)(2,1)}, u32[]{:S(2)}, u32[]{:S(2)}) async-start(bf16[8,128,512]{2,1,0:T(8,128)(2,1)} %broadcast_select_fusion.7), calls=%async_computation | async-start | bytes 2097152 | tf_op jit(solution)/shard_map/all_to_all | solution.py:28
  23.8 60.4 %all-gather.7.cloned.1.call-start = ((), (), s32[]{:S(2)}) async-start(), calls=%async_computation.6 | async-start | bytes 2621440 | tf_op jit(solution)/shard_map/all_gather | solution.py:62
  69.5 14.7 %copy-start.6 = (bf16[4,128,512]{2,1,0:T(8,128)(2,1)S(1)}, bf16[4,128,512]{2,1,0:T(8,128)(2,1)}, u32[]{:S(2)}) copy-start(bf16[4,128,512]{2,1,0:T(8,128)(2,1)} %get-tuple-element.135) | copy-start | bytes 1572868
  86.1 1.0 copy-start.1
  95.1 31.3 %all-to-all-start.1 = ((bf16[8,128,512]{2,1,0:T(8,128)(2,1)}), bf16[8,128,512]{2,1,0:T(8,128)(2,1)}, u32[]{:S(2)}, u32[]{:S(2)}) async-start(bf16[8,128,512]{2,1,0:T(8,128)(2,1)} %broadcast_select_fusion.6), calls=%async_computation.1 | async-start | bytes 2097152 | tf_op jit(solution)/shard_map/all_to_all | solution.py:28
  144.0 1.0 copy-start.2
  153.0 30.8 %all-to-all-start.2 = ((bf16[8,128,512]{2,1,0:T(8,128)(2,1)}), bf16[8,128,512]{2,1,0:T(8,128)(2,1)}, u32[]{:S(2)}, u32[]{:S(2)}) async-start(bf16[8,128,512]{2,1,0:T(8,128)(2,1)} %broadcast_select_fusion.5), calls=%async_computation.2 | async-start | bytes 2097152 | tf_op jit(solution)/shard_map/all_to_all | solution.py:28
  201.4 1.0 copy-start.4
  210.4 30.8 %all-to-all-start.3 = ((bf16[8,128,512]{2,1,0:T(8,128)(2,1)}), bf16[8,128,512]{2,1,0:T(8,128)(2,1)}, u32[]{:S(2)}, u32[]{:S(2)}) async-start(bf16[8,128,512]{2,1,0:T(8,128)(2,1)} %broadcast_select_fusion.4), calls=%async_computation.3 | async-start | bytes 2097152 | tf_op jit(solution)/shard_map/all_to_all | solution.py:28
  214.7 2.5 copy-start.3
  214.7 3.6 %copy-start.5 = (f32[512,512]{1,0:T(8,128)S(1)}, f32[512,512]{1,0:T(8,128)}, u32[]{:S(2)}) copy-start(f32[512,512]{1,0:T(8,128)} %copy-done.4) | copy-start | bytes 3145732
  258.9 1.0 copy-start.7
  258.9 1.2 copy-start.8
  258.9 1.3 copy-start.9
Sparse Core Ops, SparseCore 0:
  9.2 37.9 all-gather.4
  49.0 35.1 all-gather.6
where the time goes:
time: 298 us; the launch traced here: 296 us
  waiting for transfers between devices  87.4 us (29%)
  local copies, waits for them, and re-layouts  61.9 us (21%)
  blocking collectives  44.2 us (15%)
  matrix products  39.7 us (13%)
  other arithmetic  29.3 us (10%)
  starting transfers between devices  19.6 us (7%)
  between operations  13.7 us (5%)
    all_to_all x4, waiting for transfers between devices, sage_layer(): lax.all_to_all(outgoing, 'dom', split_axis=0, concat_axis=0, tiled=True)  73.8 us
    gather x16, local copies, waits for them, and re-layouts, block_sum(): chosen = jnp.take(sources, block_index, axis=0)  31.8 us
    all_to_all x1, blocking collectives, per_device(): lax.all_to_all(dealt_out, 'segment', split_axis=0, concat_axis=1, tiled=T...  27.8 us
    dot_general x16, matrix products, block_sum(): jnp.einsum('kij,kjd->id', masked, chosen, preferred_element_type=jnp.floa...  22.2 us
    gather x4, local copies, waits for them, and re-layouts, sage_layer(): jnp.take(inputs, send_list.reshape(-1), axis=0)  20.3 us
    all_to_all x4, starting transfers between devices, sage_layer(): lax.all_to_all(outgoing, 'dom', split_axis=0, concat_axis=0, tiled=True)  19.6 us
    all_gather x1, waiting for transfers between devices, per_device(): lax.all_gather(w_neigh, 'segment', axis=0, tiled=True)  12.2 us
    concatenate x4, other arithmetic, sage_layer(): jnp.concatenate([inputs.reshape(block_count, tile_rows, feat_width), inco...  10 us
  transfers between devices with their start and end apart: 6, of which 5 were waited for; matrix products, arithmetic and copies ran while one was open for 16% of the time, Pallas kernels for 0%

commit v1 on v0

--- a/solution.py
+++ b/solution.py
@@ -4,6 +4,18 @@
 from jax.sharding import PartitionSpec as P
 
 norm_eps = 1e-05
+
+
+def in_blocks(x, dim, size):
+    lengths = x.shape
+    blocks = x.reshape(*lengths[:dim], size, lengths[dim] // size, *lengths[dim + 1 :])
+    return jnp.moveaxis(blocks, dim, 0)
+
+
+def laid_out(pieces, dim):
+    pieces = jnp.moveaxis(pieces, 0, dim)
+    shape = pieces.shape
+    return pieces.reshape(*shape[:dim], shape[dim] * shape[dim + 1], *shape[dim + 2 :])
 
 
 def select_span(array_in, span_id):
@@ -25,7 +37,14 @@
     )
     row_live = lax.broadcasted_iota(jnp.int32, (peer_count, tile_rows), 1) < send_count[:, None]
     outgoing = jnp.where(row_live[:, :, None], picked, jnp.zeros_like(picked))
-    incoming = lax.all_to_all(outgoing, "dom", split_axis=0, concat_axis=0, tiled=True)
+    peers, index = (lax.axis_size("dom"), lax.axis_index("dom"))
+    blocks = in_blocks(outgoing, 0, peers)
+    outs = [blocks[index]]
+    for hop in range(1, peers):
+        sent = blocks[index ^ hop]
+        outs.append(lax.ppermute(sent, "dom", [(i, i ^ hop) for i in range(peers)]))
+    blocks = jnp.stack(outs)[index ^ jnp.arange(peers)]
+    incoming = laid_out(blocks, 0)
     sources = jnp.concatenate(
         [inputs.reshape(block_count, tile_rows, feat_width), incoming], axis=0
     )

time: 298 us -> 273 us (0.916)
  waiting for transfers between devices: 87.4 us -> 61.6 us
  starting transfers between devices: 19.6 us -> 41.7 us
  other arithmetic: 29.3 us -> 13.9 us
  local copies, waits for them, and re-layouts: 61.9 us -> 47.5 us
  matrix products: 39.7 us -> 44.2 us
    all_to_all x4 -> x0, waiting for transfers between devices: 73.8 us -> none  [sage_layer(): lax.all_to_all(outgoing, 'dom', split_axis=0, concat_axis=0, tiled=True)]
    ppermute x0 -> x28, waiting for transfers between devices: none -> 46.6 us  [sage_layer(): outs.append(lax.ppermute(sent, 'dom', [(i, i ^ hop) for i in range(peers)]))]
    ppermute x0 -> x28, starting transfers between devices: none -> 41.7 us  [sage_layer(): outs.append(lax.ppermute(sent, 'dom', [(i, i ^ hop) for i in range(peers)]))]
    gather x16, local copies, waits for them, and re-layouts: 31.8 us -> 9.29 us  [block_sum(): chosen = jnp.take(sources, block_index, axis=0)]
    all_to_all x4 -> x0, starting transfers between devices: 19.6 us -> none  [sage_layer(): lax.all_to_all(outgoing, 'dom', split_axis=0, concat_axis=0, tiled=True)]
    concatenate x4, other arithmetic: 10 us -> 1.78 us  [sage_layer(): jnp.concatenate([inputs.reshape(block_count, tile_rows, feat_width), inco...]
    unnamed x25 -> x71, local copies, waits for them, and re-layouts: 4.51 us -> 10.4 us
    dot_general x16, matrix products: 22.2 us -> 27.3 us  [block_sum(): jnp.einsum('kij,kjd->id', masked, chosen, preferred_element_type=jnp.floa...]
  transfers between devices with their start and end apart: 6 -> 30, of which waited for: 5 -> 10; matrix products, arithmetic and copies ran while one was open for 16% -> 16% of each run, Pallas kernels for 0% -> 0%
where the time goes in v1:
time: 273 us; the launch traced here: 269 us
  waiting for transfers between devices  61.6 us (23%)
  local copies, waits for them, and re-layouts  47.5 us (17%)
  blocking collectives  45.4 us (17%)
  matrix products  44.2 us (16%)
  starting transfers between devices  41.7 us (15%)
  between operations  14.2 us (5%)
  other arithmetic  13.9 us (5%)
    ppermute x28, waiting for transfers between devices, sage_layer(): outs.append(lax.ppermute(sent, 'dom', [(i, i ^ hop) for i in range(peers)]))  46.6 us
    ppermute x28, starting transfers between devices, sage_layer(): outs.append(lax.ppermute(sent, 'dom', [(i, i ^ hop) for i in range(peers)]))  41.7 us
    all_to_all x1, blocking collectives, per_device(): lax.all_to_all(dealt_out, 'segment', split_axis=0, concat_axis=1, tiled=T...  28.9 us
    dot_general x16, matrix products, block_sum(): jnp.einsum('kij,kjd->id', masked, chosen, preferred_element_type=jnp.floa...  27.3 us
    gather x4, local copies, waits for them, and re-layouts, sage_layer(): jnp.take(inputs, send_list.reshape(-1), axis=0)  17 us
    all_gather x1, waiting for transfers between devices, per_device(): lax.all_gather(w_neigh, 'segment', axis=0, tiled=True)  14.3 us
    unnamed x71, local copies, waits for them, and re-layouts  10.4 us
    dot_general x4, matrix products, sage_layer(): jnp.dot(inputs, w_one, preferred_element_type=jnp.float32)  9.79 us
  transfers between devices with their start and end apart: 30, of which 10 were waited for; matrix products, arithmetic and copies ran while one was open for 16% of the time, Pallas kernels for 0%

profile of v1, /device:TPU:0, one launch (start us, length us, event | category | flops | bytes accessed | tf_op | source)
XLA Modules:
  0.0 269.0 jit_solution(9044457115183121006)
XLA Ops:
  8.2 5.1 %gather_fusion.8 = bf16[1024,512]{1,0:T(8,128)(2,1)} fusion(bf16[512,512]{1,0:T(8,128)(2,1)S(1)} %fusion.70, s32[1024]{0:T(1024)S(1)} %fusion.50), kind=kCustom, calls=%fused_computation.clone | custom fusion | bytes 2101248 | tf_op jit(solution)/shard_map/jit(_take)/gather | solution.py:35
  20.6 2.8 %collective-permute-start.3 = (bf16[1,128,512]{2,1,0:T(8,128)(2,1)S(1)}, bf16[1,128,512]{2,1,0:T(8,128)(2,1)}, u32[]{:S(2)}, u32[]{:S(2)}) collective-permute-start(bf16[1,128,512]{2,1,0:T(8,128)(2,1)S(1)} %get-tuple-element.219), channel_id=1, source_target_pairs={{0,4},{1,5},{2,6},{3,7},{4,0},{5,1},{6,2},{7,3},{8,12},{9,13},{10,... | collective-permute-start | bytes 393224 | tf_op jit(solution)/shard_map/ppermute | solution.py:45
  25.7 8.1 %all-gather = bf16[4,1,512]{2,1,0:T(2,128)(2,1)S(1)} all-gather(bf16[1,1,512]{2,1,0:T(2,128)(2,1)S(1)} %bitcast.279), channel_id=1, replica_groups=mesh['segment'=4,'dom'=8] {'segment'}, dimensions={0}, use_global_device_ids=true | all-gather | bytes 5120 | tf_op jit(solution)/shard_map/all_gather | solution.py:82
  34.5 8.4 %all-gather.1 = bf16[4,1,512]{2,1,0:T(2,128)(2,1)S(1)} all-gather(bf16[1,1,512]{2,1,0:T(2,128)(2,1)} %bitcast.280), channel_id=1, replica_groups=mesh['segment'=4,'dom'=8] {'segment'}, dimensions={0}, use_global_device_ids=true | all-gather | bytes 5120 | tf_op jit(solution)/shard_map/all_gather | solution.py:83
  46.0 3.6 %collective-permute-start.5 = (bf16[1,128,512]{2,1,0:T(8,128)(2,1)S(1)}, bf16[1,128,512]{2,1,0:T(8,128)(2,1)S(1)}, u32[]{:S(2)}, u32[]{:S(2)}) collective-permute-start(bf16[1,128,512]{2,1,0:T(8,128)(2,1)S(1)} %get-tuple-element.217), channel_id=1, source_target_pairs={{0,6},{1,7},{2,4},{3,5},{4,2},{5,3},{6,0},{7,1},{8,14},{9,15},{10,... | collective-permute-start | bytes 393224 | tf_op jit(solution)/shard_map/ppermute | solution.py:45
  59.9 7.5 %while.40 = (s32[]{:T(128)}, bf16[4,128,512]{2,1,0:T(8,128)(2,1)S(1)}, pred[4,4]{1,0:T(4,128)(4,1)S(1)}, bf16[4,4,128,128]{3,2,1,0:T(8,128)(2,1)}, s32[4,4]{1,0:...) while((s32[]{:T(128)}, bf16[4,128,512]{2,1,0:T(8,128)(2,1)S(1)}, pred[4,4]{1,0:T(4,128)(4,1)S(1)}, ...), condition=%wide.region_1.4_spmd, body=%wide.region_0.3_spmd.sunk | while | flops 67437592 | bytes 1972385 | solution.py:59
  69.9 14.3 %all-gather.7.cloned.1.call-done = bf16[4,512,512]{2,1,0:T(8,128)(2,1)} async-done(((bf16[1,512,512]{2,1,0:T(8,128)(2,1)}), bf16[4,512,512]{2,1,0:T(8,128)(2,1)}) %all-gather.7.cloned.1.call-update) | async-done | bytes 2097168 | tf_op jit(solution)/shard_map/all_gather | solution.py:81
  86.7 4.0 %gather_fusion.9 = bf16[1024,512]{1,0:T(8,128)(2,1)S(1)} fusion(bf16[512,512]{1,0:T(8,128)(2,1)S(1)} %maximum_convert_fusion.3, s32[1024]{0:T(1024)S(1)} %fusion.50), kind=kCustom, calls=%fused_computation.2.clone | custom fusion | bytes 2101248 | tf_op jit(solution)/shard_map/jit(_take)/gather | solution.py:35
  99.7 3.4 %collective-permute-start.12 = (bf16[1,128,512]{2,1,0:T(8,128)(2,1)S(1)}, bf16[1,128,512]{2,1,0:T(8,128)(2,1)S(1)}, u32[]{:S(2)}, u32[]{:S(2)}) collective-permute-start(bf16[1,128,512]{2,1,0:T(8,128)(2,1)S(1)} %get-tuple-element.210), channel_id=1, source_target_pairs={{0,6},{1,7},{2,4},{3,5},{4,2},{5,3},{6,0},{7,1},{8,14},{9,15},{10,... | collective-permute-start | bytes 393224 | tf_op jit(solution)/shard_map/ppermute | solution.py:45
  103.1 3.5 %collective-permute-done.8 = bf16[1,128,512]{2,1,0:T(8,128)(2,1)S(1)} collective-permute-done((bf16[1,128,512]{2,1,0:T(8,128)(2,1)S(1)}, bf16[1,128,512]{2,1,0:T(8,128)(2,1)S(1)}, u32[]{:S(2)}, u32[]{:S(2)}) %collective-permute-start.8) | collective-permute-done | bytes 131104 | tf_op jit(solution)/shard_map/ppermute | solution.py:45
  108.5 8.9 %collective-permute-done.11 = bf16[1,128,512]{2,1,0:T(8,128)(2,1)S(1)} collective-permute-done((bf16[1,128,512]{2,1,0:T(8,128)(2,1)S(1)}, bf16[1,128,512]{2,1,0:T(8,128)(2,1)S(1)}, u32[]{:S(2)}, u32[]{:S(2)}) %collective-permute-start.11) | collective-permute-done | bytes 131104 | tf_op jit(solution)/shard_map/ppermute | solution.py:45
  119.2 10.0 %while.41 = (s32[]{:T(128)}, bf16[4,128,512]{2,1,0:T(8,128)(2,1)}, pred[4,4]{1,0:T(4,128)(4,1)S(1)}, bf16[4,4,128,128]{3,2,1,0:T(8,128)(2,1)}, s32[4,4]{1,0:T(4,...) while((s32[]{:T(128)}, bf16[4,128,512]{2,1,0:T(8,128)(2,1)}, pred[4,4]{1,0:T(4,128)(4,1)S(1)}, ...), condition=%wide.region_5.8_spmd, body=%wide.region_4.7_spmd.sunk | while | flops 67437592 | bytes 1971369 | solution.py:59
  131.6 4.0 %gather_fusion.10 = bf16[1024,512]{1,0:T(8,128)(2,1)S(1)} fusion(bf16[512,512]{1,0:T(8,128)(2,1)S(1)} %maximum_convert_fusion.2, s32[1024]{0:T(1024)S(1)} %fusion.50), kind=kCustom, calls=%fused_computation.3.clone | custom fusion | bytes 2101248 | tf_op jit(solution)/shard_map/jit(_take)/gather | solution.py:35
  140.2 5.9 %collective-permute-start.15 = (bf16[1,128,512]{2,1,0:T(8,128)(2,1)S(1)}, bf16[1,128,512]{2,1,0:T(8,128)(2,1)S(1)}, u32[]{:S(2)}, u32[]{:S(2)}) collective-permute-start(bf16[1,128,512]{2,1,0:T(8,128)(2,1)S(1)} %get-tuple-element.207), channel_id=1, source_target_pairs={{0,2},{1,3},{2,0},{3,1},{4,6},{5,7},{6,4},{7,5},{8,10},{9,11},{10,... | collective-permute-start | bytes 393224 | tf_op jit(solution)/shard_map/ppermute | solution.py:45
  146.2 3.0 %collective-permute-start.17 = (bf16[1,128,512]{2,1,0:T(8,128)(2,1)S(1)}, bf16[1,128,512]{2,1,0:T(8,128)(2,1)S(1)}, u32[]{:S(2)}, u32[]{:S(2)}) collective-permute-start(bf16[1,128,512]{2,1,0:T(8,128)(2,1)S(1)} %get-tuple-element.205), channel_id=1, source_target_pairs={{0,4},{1,5},{2,6},{3,7},{4,0},{5,1},{6,2},{7,3},{8,12},{9,13},{10,... | collective-permute-start | bytes 393224 | tf_op jit(solution)/shard_map/ppermute | solution.py:45
  153.0 4.6 %collective-permute-done.16 = bf16[1,128,512]{2,1,0:T(8,128)(2,1)S(1)} collective-permute-done((bf16[1,128,512]{2,1,0:T(8,128)(2,1)S(1)}, bf16[1,128,512]{2,1,0:T(8,128)(2,1)S(1)}, u32[]{:S(2)}, u32[]{:S(2)}) %collective-permute-start.16) | collective-permute-done | bytes 131104 | tf_op jit(solution)/shard_map/ppermute | solution.py:45
  157.7 9.7 %collective-permute-done.18 = bf16[1,128,512]{2,1,0:T(8,128)(2,1)S(1)} collective-permute-done((bf16[1,128,512]{2,1,0:T(8,128)(2,1)S(1)}, bf16[1,128,512]{2,1,0:T(8,128)(2,1)S(1)}, u32[]{:S(2)}, u32[]{:S(2)}) %collective-permute-start.18) | collective-permute-done | bytes 131104 | tf_op jit(solution)/shard_map/ppermute | solution.py:45
  169.3 10.0 %while.42 = (s32[]{:T(128)}, bf16[4,128,512]{2,1,0:T(8,128)(2,1)}, pred[4,4]{1,0:T(4,128)(4,1)S(1)}, bf16[4,4,128,128]{3,2,1,0:T(8,128)(2,1)}, s32[4,4]{1,0:T(4,...) while((s32[]{:T(128)}, bf16[4,128,512]{2,1,0:T(8,128)(2,1)}, pred[4,4]{1,0:T(4,128)(4,1)S(1)}, ...), condition=%wide.region_9.12_spmd, body=%wide.region_8.11_spmd.sunk | while | flops 67437592 | bytes 1971369 | solution.py:59
  181.6 4.0 %gather_fusion.11 = bf16[1024,512]{1,0:T(8,128)(2,1)S(1)} fusion(bf16[512,512]{1,0:T(8,128)(2,1)S(1)} %maximum_convert_fusion.1, s32[1024]{0:T(1024)S(1)} %fusion.50), kind=kCustom, calls=%fused_computation.4.clone | custom fusion | bytes 2101248 | tf_op jit(solution)/shard_map/jit(_take)/gather | solution.py:35
  189.8 6.1 %collective-permute-start.22 = (bf16[1,128,512]{2,1,0:T(8,128)(2,1)S(1)}, bf16[1,128,512]{2,1,0:T(8,128)(2,1)S(1)}, u32[]{:S(2)}, u32[]{:S(2)}) collective-permute-start(bf16[1,128,512]{2,1,0:T(8,128)(2,1)S(1)} %get-tuple-element.200), channel_id=1, source_target_pairs={{0,2},{1,3},{2,0},{3,1},{4,6},{5,7},{6,4},{7,5},{8,10},{9,11},{10,... | collective-permute-start | bytes 393224 | tf_op jit(solution)/shard_map/ppermute | solution.py:45
  200.4 4.1 %collective-permute-done.22 = bf16[1,128,512]{2,1,0:T(8,128)(2,1)S(1)} collective-permute-done((bf16[1,128,512]{2,1,0:T(8,128)(2,1)S(1)}, bf16[1,128,512]{2,1,0:T(8,128)(2,1)S(1)}, u32[]{:S(2)}, u32[]{:S(2)}) %collective-permute-start.22) | collective-permute-done | bytes 131104 | tf_op jit(solution)/shard_map/ppermute | solution.py:45
  207.2 8.6 %collective-permute-done.25 = bf16[1,128,512]{2,1,0:T(8,128)(2,1)S(1)} collective-permute-done((bf16[1,128,512]{2,1,0:T(8,128)(2,1)S(1)}, bf16[1,128,512]{2,1,0:T(8,128)(2,1)S(1)}, u32[]{:S(2)}, u32[]{:S(2)}) %collective-permute-start.25) | collective-permute-done | bytes 131104 | tf_op jit(solution)/shard_map/ppermute | solution.py:45
  217.5 10.0 %while.43 = (s32[]{:T(128)}, bf16[4,128,512]{2,1,0:T(8,128)(2,1)}, pred[4,4]{1,0:T(4,128)(4,1)S(1)}, bf16[4,4,128,128]{3,2,1,0:T(8,128)(2,1)}, s32[4,4]{1,0:T(4,...) while((s32[]{:T(128)}, bf16[4,128,512]{2,1,0:T(8,128)(2,1)}, pred[4,4]{1,0:T(4,128)(4,1)S(1)}, ...), condition=%wide.region_13.16_spmd, body=%wide.region_12.15_spmd.sunk | while | flops 67437592 | bytes 1971369 | solution.py:59
  230.9 28.9 %all_to_all.12 = bf16[4,1,512,512]{3,2,1,0:T(8,128)(2,1)S(1)} all-to-all(bf16[4,1,512,512]{3,2,1,0:T(8,128)(2,1)S(1)} %maximum_bitcast_fusion), channel_id=1, replica_groups=mesh['segment'=4,'dom'=8] {'segment'}, dimensions={0} | all-to-all | bytes 4194304 | tf_op jit(solution)/shard_map/all_to_all | solution.py:103
  (270 shorter events, 113.4 us)
Async XLA Ops:
  6.5 60.9 %all-gather.5.cloned.1.call-start = ((), (), s32[]{:S(2)}) async-start(), calls=%async_computation.1 | async-start | bytes 2621440 | tf_op jit(solution)/shard_map/all_gather | solution.py:80
  7.3 77.0 %all-gather.7.cloned.1.call-start = ((), (), s32[]{:S(2)}) async-start(), calls=%async_computation.2 | async-start | bytes 2621440 | tf_op jit(solution)/shard_map/all_gather | solution.py:81
  17.4 28.6 %collective-permute-start = (bf16[1,128,512]{2,1,0:T(8,128)(2,1)S(1)}, bf16[1,128,512]{2,1,0:T(8,128)(2,1)}, u32[]{:S(2)}, u32[]{:S(2)}) collective-permute-start(bf16[1,128,512]{2,1,0:T(8,128)(2,1)S(1)} %get-tuple-element.222), channel_id=1, source_target_pairs={{0,1},{1,0},{2,3},{3,2},{4,5},{5,4},{6,7},{7,6},{8,9},{9,8},{10,11... | collective-permute-start | bytes 393224 | tf_op jit(solution)/shard_map/ppermute | solution.py:45
  17.9 32.6 %collective-permute-start.1 = (bf16[1,128,512]{2,1,0:T(8,128)(2,1)S(1)}, bf16[1,128,512]{2,1,0:T(8,128)(2,1)}, u32[]{:S(2)}, u32[]{:S(2)}) collective-permute-start(bf16[1,128,512]{2,1,0:T(8,128)(2,1)S(1)} %get-tuple-element.221), channel_id=1, source_target_pairs={{0,2},{1,3},{2,0},{3,1},{4,6},{5,7},{6,4},{7,5},{8,10},{9,11},{10,... | collective-permute-start | bytes 393224 | tf_op jit(solution)/shard_map/ppermute | solution.py:45
  20.6 31.0 %collective-permute-start.2 = (bf16[1,128,512]{2,1,0:T(8,128)(2,1)S(1)}, bf16[1,128,512]{2,1,0:T(8,128)(2,1)}, u32[]{:S(2)}, u32[]{:S(2)}) collective-permute-start(bf16[1,128,512]{2,1,0:T(8,128)(2,1)S(1)} %get-tuple-element.220), channel_id=1, source_target_pairs={{0,3},{1,2},{2,1},{3,0},{4,7},{5,6},{6,5},{7,4},{8,11},{9,10},{10,... | collective-permute-start | bytes 393224 | tf_op jit(solution)/shard_map/ppermute | solution.py:45
  20.6 31.9 %collective-permute-start.3 = (bf16[1,128,512]{2,1,0:T(8,128)(2,1)S(1)}, bf16[1,128,512]{2,1,0:T(8,128)(2,1)}, u32[]{:S(2)}, u32[]{:S(2)}) collective-permute-start(bf16[1,128,512]{2,1,0:T(8,128)(2,1)S(1)} %get-tuple-element.219), channel_id=1, source_target_pairs={{0,4},{1,5},{2,6},{3,7},{4,0},{5,1},{6,2},{7,3},{8,12},{9,13},{10,... | collective-permute-start | bytes 393224 | tf_op jit(solution)/shard_map/ppermute | solution.py:45
  23.4 30.0 %collective-permute-start.4 = (bf16[1,128,512]{2,1,0:T(8,128)(2,1)S(1)}, bf16[1,128,512]{2,1,0:T(8,128)(2,1)}, u32[]{:S(2)}, u32[]{:S(2)}) collective-permute-start(bf16[1,128,512]{2,1,0:T(8,128)(2,1)S(1)} %get-tuple-element.218), channel_id=1, source_target_pairs={{0,5},{1,4},{2,7},{3,6},{4,1},{5,0},{6,3},{7,2},{8,13},{9,12},{10,... | collective-permute-start | bytes 393224 | tf_op jit(solution)/shard_map/ppermute | solution.py:45
  95.2 11.3 %collective-permute-start.8 = (bf16[1,128,512]{2,1,0:T(8,128)(2,1)S(1)}, bf16[1,128,512]{2,1,0:T(8,128)(2,1)S(1)}, u32[]{:S(2)}, u32[]{:S(2)}) collective-permute-start(bf16[1,128,512]{2,1,0:T(8,128)(2,1)S(1)} %get-tuple-element.214), channel_id=1, source_target_pairs={{0,2},{1,3},{2,0},{3,1},{4,6},{5,7},{6,4},{7,5},{8,10},{9,11},{10,... | collective-permute-start | bytes 393224 | tf_op jit(solution)/shard_map/ppermute | solution.py:45
  96.7 11.7 %collective-permute-start.9 = (bf16[1,128,512]{2,1,0:T(8,128)(2,1)S(1)}, bf16[1,128,512]{2,1,0:T(8,128)(2,1)S(1)}, u32[]{:S(2)}, u32[]{:S(2)}) collective-permute-start(bf16[1,128,512]{2,1,0:T(8,128)(2,1)S(1)} %get-tuple-element.213), channel_id=1, source_target_pairs={{0,3},{1,2},{2,1},{3,0},{4,7},{5,6},{6,5},{7,4},{8,11},{9,10},{10,... | collective-permute-start | bytes 393224 | tf_op jit(solution)/shard_map/ppermute | solution.py:45
  97.1 11.4 %collective-permute-start.10 = (bf16[1,128,512]{2,1,0:T(8,128)(2,1)S(1)}, bf16[1,128,512]{2,1,0:T(8,128)(2,1)S(1)}, u32[]{:S(2)}, u32[]{:S(2)}) collective-permute-start(bf16[1,128,512]{2,1,0:T(8,128)(2,1)S(1)} %get-tuple-element.212), channel_id=1, source_target_pairs={{0,4},{1,5},{2,6},{3,7},{4,0},{5,1},{6,2},{7,3},{8,12},{9,13},{10,... | collective-permute-start | bytes 393224 | tf_op jit(solution)/shard_map/ppermute | solution.py:45
  99.5 17.9 %collective-permute-start.11 = (bf16[1,128,512]{2,1,0:T(8,128)(2,1)S(1)}, bf16[1,128,512]{2,1,0:T(8,128)(2,1)S(1)}, u32[]{:S(2)}, u32[]{:S(2)}) collective-permute-start(bf16[1,128,512]{2,1,0:T(8,128)(2,1)S(1)} %get-tuple-element.211), channel_id=1, source_target_pairs={{0,5},{1,4},{2,7},{3,6},{4,1},{5,0},{6,3},{7,2},{8,13},{9,12},{10,... | collective-permute-start | bytes 393224 | tf_op jit(solution)/shard_map/ppermute | solution.py:45
  99.7 17.8 %collective-permute-start.12 = (bf16[1,128,512]{2,1,0:T(8,128)(2,1)S(1)}, bf16[1,128,512]{2,1,0:T(8,128)(2,1)S(1)}, u32[]{:S(2)}, u32[]{:S(2)}) collective-permute-start(bf16[1,128,512]{2,1,0:T(8,128)(2,1)S(1)} %get-tuple-element.210), channel_id=1, source_target_pairs={{0,6},{1,7},{2,4},{3,5},{4,2},{5,3},{6,0},{7,1},{8,14},{9,15},{10,... | collective-permute-start | bytes 393224 | tf_op jit(solution)/shard_map/ppermute | solution.py:45
  136.0 13.5 %collective-permute-start.14 = (bf16[1,128,512]{2,1,0:T(8,128)(2,1)S(1)}, bf16[1,128,512]{2,1,0:T(8,128)(2,1)S(1)}, u32[]{:S(2)}, u32[]{:S(2)}) collective-permute-start(bf16[1,128,512]{2,1,0:T(8,128)(2,1)S(1)} %get-tuple-element.208), channel_id=1, source_target_pairs={{0,1},{1,0},{2,3},{3,2},{4,5},{5,4},{6,7},{7,6},{8,9},{9,8},{10,11... | collective-permute-start | bytes 393224 | tf_op jit(solution)/shard_map/ppermute | solution.py:45
  140.2 11.6 %collective-permute-start.15 = (bf16[1,128,512]{2,1,0:T(8,128)(2,1)S(1)}, bf16[1,128,512]{2,1,0:T(8,128)(2,1)S(1)}, u32[]{:S(2)}, u32[]{:S(2)}) collective-permute-start(bf16[1,128,512]{2,1,0:T(8,128)(2,1)S(1)} %get-tuple-element.207), channel_id=1, source_target_pairs={{0,2},{1,3},{2,0},{3,1},{4,6},{5,7},{6,4},{7,5},{8,10},{9,11},{10,... | collective-permute-start | bytes 393224 | tf_op jit(solution)/shard_map/ppermute | solution.py:45
  146.1 11.6 %collective-permute-start.16 = (bf16[1,128,512]{2,1,0:T(8,128)(2,1)S(1)}, bf16[1,128,512]{2,1,0:T(8,128)(2,1)S(1)}, u32[]{:S(2)}, u32[]{:S(2)}) collective-permute-start(bf16[1,128,512]{2,1,0:T(8,128)(2,1)S(1)} %get-tuple-element.206), channel_id=1, source_target_pairs={{0,3},{1,2},{2,1},{3,0},{4,7},{5,6},{6,5},{7,4},{8,11},{9,10},{10,... | collective-permute-start | bytes 393224 | tf_op jit(solution)/shard_map/ppermute | solution.py:45
  146.2 11.5 %collective-permute-start.17 = (bf16[1,128,512]{2,1,0:T(8,128)(2,1)S(1)}, bf16[1,128,512]{2,1,0:T(8,128)(2,1)S(1)}, u32[]{:S(2)}, u32[]{:S(2)}) collective-permute-start(bf16[1,128,512]{2,1,0:T(8,128)(2,1)S(1)} %get-tuple-element.205), channel_id=1, source_target_pairs={{0,4},{1,5},{2,6},{3,7},{4,0},{5,1},{6,2},{7,3},{8,12},{9,13},{10,... | collective-permute-start | bytes 393224 | tf_op jit(solution)/shard_map/ppermute | solution.py:45
  149.2 18.3 %collective-permute-start.18 = (bf16[1,128,512]{2,1,0:T(8,128)(2,1)S(1)}, bf16[1,128,512]{2,1,0:T(8,128)(2,1)S(1)}, u32[]{:S(2)}, u32[]{:S(2)}) collective-permute-start(bf16[1,128,512]{2,1,0:T(8,128)(2,1)S(1)} %get-tuple-element.204), channel_id=1, source_target_pairs={{0,5},{1,4},{2,7},{3,6},{4,1},{5,0},{6,3},{7,2},{8,13},{9,12},{10,... | collective-permute-start | bytes 393224 | tf_op jit(solution)/shard_map/ppermute | solution.py:45
  149.6 17.9 %collective-permute-start.19 = (bf16[1,128,512]{2,1,0:T(8,128)(2,1)S(1)}, bf16[1,128,512]{2,1,0:T(8,128)(2,1)S(1)}, u32[]{:S(2)}, u32[]{:S(2)}) collective-permute-start(bf16[1,128,512]{2,1,0:T(8,128)(2,1)S(1)} %get-tuple-element.203), channel_id=1, source_target_pairs={{0,6},{1,7},{2,4},{3,5},{4,2},{5,3},{6,0},{7,1},{8,14},{9,15},{10,... | collective-permute-start | bytes 393224 | tf_op jit(solution)/shard_map/ppermute | solution.py:45
  151.7 15.7 %collective-permute-start.20 = (bf16[1,128,512]{2,1,0:T(8,128)(2,1)S(1)}, bf16[1,128,512]{2,1,0:T(8,128)(2,1)S(1)}, u32[]{:S(2)}, u32[]{:S(2)}) collective-permute-start(bf16[1,128,512]{2,1,0:T(8,128)(2,1)S(1)} %get-tuple-element.202), channel_id=1, source_target_pairs={{0,7},{1,6},{2,5},{3,4},{4,3},{5,2},{6,1},{7,0},{8,15},{9,14},{10,... | collective-permute-start | bytes 393224 | tf_op jit(solution)/shard_map/ppermute | solution.py:45
  186.1 12.2 %collective-permute-start.21 = (bf16[1,128,512]{2,1,0:T(8,128)(2,1)S(1)}, bf16[1,128,512]{2,1,0:T(8,128)(2,1)S(1)}, u32[]{:S(2)}, u32[]{:S(2)}) collective-permute-start(bf16[1,128,512]{2,1,0:T(8,128)(2,1)S(1)} %get-tuple-element.201), channel_id=1, source_target_pairs={{0,1},{1,0},{2,3},{3,2},{4,5},{5,4},{6,7},{7,6},{8,9},{9,8},{10,11... | collective-permute-start | bytes 393224 | tf_op jit(solution)/shard_map/ppermute | solution.py:45
  189.8 14.7 %collective-permute-start.22 = (bf16[1,128,512]{2,1,0:T(8,128)(2,1)S(1)}, bf16[1,128,512]{2,1,0:T(8,128)(2,1)S(1)}, u32[]{:S(2)}, u32[]{:S(2)}) collective-permute-start(bf16[1,128,512]{2,1,0:T(8,128)(2,1)S(1)} %get-tuple-element.200), channel_id=1, source_target_pairs={{0,2},{1,3},{2,0},{3,1},{4,6},{5,7},{6,4},{7,5},{8,10},{9,11},{10,... | collective-permute-start | bytes 393224 | tf_op jit(solution)/shard_map/ppermute | solution.py:45
  197.8 17.9 %collective-permute-start.25 = (bf16[1,128,512]{2,1,0:T(8,128)(2,1)S(1)}, bf16[1,128,512]{2,1,0:T(8,128)(2,1)S(1)}, u32[]{:S(2)}, u32[]{:S(2)}) collective-permute-start(bf16[1,128,512]{2,1,0:T(8,128)(2,1)S(1)} %get-tuple-element.197), channel_id=1, source_target_pairs={{0,5},{1,4},{2,7},{3,6},{4,1},{5,0},{6,3},{7,2},{8,13},{9,12},{10,... | collective-permute-start | bytes 393224 | tf_op jit(solution)/shard_map/ppermute | solution.py:45
  198.3 17.5 %collective-permute-start.26 = (bf16[1,128,512]{2,1,0:T(8,128)(2,1)S(1)}, bf16[1,128,512]{2,1,0:T(8,128)(2,1)S(1)}, u32[]{:S(2)}, u32[]{:S(2)}) collective-permute-start(bf16[1,128,512]{2,1,0:T(8,128)(2,1)S(1)} %get-tuple-element.196), channel_id=1, source_target_pairs={{0,6},{1,7},{2,4},{3,5},{4,2},{5,3},{6,0},{7,1},{8,14},{9,15},{10,... | collective-permute-start | bytes 393224 | tf_op jit(solution)/shard_map/ppermute | solution.py:45
  204.5 11.3 %collective-permute-start.27 = (bf16[1,128,512]{2,1,0:T(8,128)(2,1)S(1)}, bf16[1,128,512]{2,1,0:T(8,128)(2,1)S(1)}, u32[]{:S(2)}, u32[]{:S(2)}) collective-permute-start(bf16[1,128,512]{2,1,0:T(8,128)(2,1)S(1)} %get-tuple-element.195), channel_id=1, source_target_pairs={{0,7},{1,6},{2,5},{3,4},{4,3},{5,2},{6,1},{7,0},{8,15},{9,14},{10,... | collective-permute-start | bytes 393224 | tf_op jit(solution)/shard_map/ppermute | solution.py:45
  (27 other events, 155.4 us)
Sparse Core Ops, SparseCore 0:
  9.2 37.9 all-gather.4
  49.0 35.1 all-gather.6
